TPU v7x, 128 devices: a whole 4x4x4 slice. The times are simulated.
128 devices in a mesh: grid: 16 (over y, z), blk: 8 (over x, core).
Axes of the slice: x: 4, y: 4, z: 4, core: 2. Of those that a mesh axis runs over, the one named last changes fastest.
Arguments:
- a_slots: bfloat16 [16, 8, 16, 2, 128, 128], P('grid', 'blk'), may hold values from -6 to 6
- a_rows: int32 [16, 8, 16, 2], P('grid', 'blk'), may hold values from 0 to 127, as said below
- a_cols: int32 [16, 8, 16, 2], P('grid', 'blk'), may hold values from 0 to 63
- a_count: int32 [16, 8, 16], P('grid', 'blk'), may hold values from 0 to 2, as said below
- owned_rows: int32 [16, 8], P('grid'), may hold values from 0 to 127, as said below
- b_matrix: bfloat16 [8192, 8192], P('grid', 'blk'), may hold values from -0.125 to 0.125
Outputs:
- product: bfloat16 [16384, 8192], P('grid', 'blk')
Inputs may be any that keep to these rules, and one draw needn't show every extreme that they name: `a_rows`: every slot sent to product owner g, live or padded, names one of the block rows owned_rows[g, 0 .. 7]; no two slots of the whole draw name the same block row and block column. `a_count`: some product owner receives 2 live slots from every atom owner and atom column. `owned_rows`: A permutation of the 128 block rows.
All inputs are finite; a program needn't handle non-finite values.
Results may differ from a plain program's by a relative error of at most 0.001.
Values may be sent and summed in bfloat16 or wider, within the bound.
A program may use at most 128 MiB of HBM per device.

v0:
```python
import jax
import jax.numpy as jnp
from jax import lax
from jax.sharding import PartitionSpec as P

CAP = 2
RB = 8


def body(a_slots, a_rows, a_cols, a_count, owned_rows, b_matrix):
    groups = lax.axis_size("grid")
    columns = lax.axis_size("blk")
    block_size = a_slots.shape[-1]
    landed = (
        lax.all_to_all(
            a_slots.reshape(groups, CAP, block_size, block_size),
            "grid",
            split_axis=0,
            concat_axis=0,
            tiled=True,
        ),
        lax.all_to_all(
            a_rows.reshape(groups, CAP), "grid", split_axis=0, concat_axis=0, tiled=True
        ),
        lax.all_to_all(
            a_cols.reshape(groups, CAP), "grid", split_axis=0, concat_axis=0, tiled=True
        ),
        lax.all_to_all(a_count.reshape(groups, 1), "grid", split_axis=0, concat_axis=0, tiled=True),
    )
    slot_data, slot_rows, slot_cols, slot_count = (
        lax.all_gather(landed[0][None], "blk", axis=0, tiled=True),
        lax.all_gather(landed[1][None], "blk", axis=0, tiled=True),
        lax.all_gather(landed[2][None], "blk", axis=0, tiled=True),
        lax.all_gather(landed[3][None], "blk", axis=0, tiled=True),
    )
    total = columns * groups * CAP
    live = (jnp.arange(CAP, dtype=jnp.int32)[None, None, :] < slot_count).reshape(total)
    slot_rows = slot_rows.reshape(total)
    slot_cols = slot_cols.reshape(total)
    slot_data = slot_data.reshape(total, block_size, block_size)
    owned = owned_rows.reshape(RB)
    row_hit = (slot_rows[:, None] == owned[None, :]) & live[:, None]
    k_blocks = b_matrix.shape[0] * groups // block_size
    col_hit = slot_cols[:, None] == jnp.arange(k_blocks, dtype=jnp.int32)[None, :]
    placing = (
        (row_hit[:, :, None] & col_hit[:, None, :])
        .reshape(total, RB * k_blocks)
        .astype(jnp.bfloat16)
    )
    spread = jnp.einsum(
        "sp,sq->pq",
        placing,
        slot_data.reshape(total, block_size * block_size),
        preferred_element_type=jnp.float32,
    )
    tile = spread.astype(jnp.bfloat16).reshape(RB, k_blocks, block_size, block_size)
    tile = tile.transpose(0, 2, 1, 3).reshape(RB * block_size, k_blocks * block_size)
    result = jnp.dot(
        tile,
        lax.all_gather(b_matrix, "grid", axis=0, tiled=True),
        preferred_element_type=jnp.float32,
    )
    return result.astype(jnp.bfloat16)


def solution(mesh):
    in_specs = (
        P("grid", "blk", None, None, None, None),
        P("grid", "blk", None, None),
        P("grid", "blk", None, None),
        P("grid", "blk", None),
        P("grid", None),
        P("grid", "blk"),
    )
    out_specs = P("grid", "blk")
    return jax.shard_map(body, mesh=mesh, in_specs=in_specs, out_specs=out_specs, check_vma=False)
```

profile of v0, /device:TPU:1, one launch (start us, length us, event | category | flops | bytes accessed | tf_op | source)
XLA Modules:
  0.0 225.2 jit_solution(14155272657976014603)
XLA Ops:
  6.5 24.6 %all_to_all.32 = bf16[16,2,128,128]{3,2,1,0:T(8,128)(2,1)} all-to-all(bf16[16,2,128,128]{3,2,1,0:T(8,128)(2,1)} %bitcast.31), channel_id=1, replica_groups=mesh['grid'=16,'blk'=8] {'grid'}, dimensions={0} | all-to-all | bytes 2097152 | tf_op jit(solution)/shard_map/all_to_all | solution.py:15
  31.2 0.7 all-gather.7.cloned.1.call-update
  31.9 1.3 copy.15
  33.2 3.6 %all-to-all-start.1 = ((s32[16,1,1]{2,1,0:T(1,128)}), s32[16,1,1]{2,1,0:T(1,128)S(1)}, u32[]{:S(2)}, u32[]{:S(2)}) async-start(s32[16,1,1]{2,1,0:T(1,128)} %copy.15), calls=%async_computation.1 | async-start | bytes 16384 | tf_op jit(solution)/shard_map/all_to_all | solution.py:28
  36.9 1.3 copy.14
  38.2 1.4 copy.16
  39.6 1.3 dynamic-slice
  41.5 1.8 all-to-all-done.1
  43.3 4.9 %all-to-all-start = ((s32[16,1,2]{2,1,0:T(1,128)}), s32[16,1,2]{2,1,0:T(1,128)S(1)}, u32[]{:S(2)}, u32[]{:S(2)}) async-start(s32[16,1,2]{2,1,0:T(1,128)} %copy.14), calls=%async_computation | async-start | bytes 16384 | tf_op jit(solution)/shard_map/all_to_all | solution.py:22
  48.1 0.4 reduce.1
  48.5 0.2 dynamic-update-slice
  48.8 10.3 %all-reduce = s32[128]{0:T(128)S(1)} all-reduce(s32[128]{0:T(128)S(1)} %dynamic-update-slice), channel_id=3, replica_groups=mesh['grid'=16,'blk'=8] {'blk'}, use_global_device_ids=true, to_apply=%add | all-reduce | flops 128 | bytes 1024
  59.4 6.9 %all-to-all-start.2 = ((s32[16,1,2]{2,1,0:T(1,128)}), s32[16,1,2]{2,1,0:T(1,128)S(1)}, u32[]{:S(2)}, u32[]{:S(2)}) async-start(s32[16,1,2]{2,1,0:T(1,128)} %copy.16), calls=%async_computation.2 | async-start | bytes 16384 | tf_op jit(solution)/shard_map/all_to_all | solution.py:25
  66.3 14.7 %all-gather = s32[128,1,2]{2,1,0:T(1,128)S(1)} all-gather(s32[16,1,2]{2,1,0:T(1,128)S(1)} %all-to-all-done), channel_id=2, replica_groups=mesh['grid'=16,'blk'=8] {'blk'}, dimensions={0}, use_global_device_ids=true | all-gather | bytes 1152 | tf_op jit(solution)/shard_map/all_gather | solution.py:32
  81.0 0.6 broadcast.56
  81.6 0.8 reduce.8
  82.6 12.8 %all-gather.2 = s32[128,1,2]{2,1,0:T(1,128)S(1)} all-gather(s32[16,1,2]{2,1,0:T(1,128)S(1)} %all-to-all-done.2), channel_id=4, replica_groups=mesh['grid'=16,'blk'=8] {'blk'}, dimensions={0}, use_global_device_ids=true | all-gather | bytes 1152 | tf_op jit(solution)/shard_map/all_gather | solution.py:33
  95.4 0.9 reduce.7
  96.4 0.7 compare_and_fusion
  97.2 18.5 %fusion.5 = bf16[64,8,128,128]{3,1,2,0:T(8,128)(2,1)} fusion(pred[256,512]{0,1:T(32,128)(4,1)S(1)} %bitcast.32, bf16[32,8,128,128]{3,2,1,0:T(8,128)(2,1)} %bitcast.30), kind=kOutput, calls=%fused_computation.6 | convolution fusion | flops 4303355904 | bytes 25296896 | tf_op jit(solution)/shard_map/sp,sq->pq/dot_general | solution.py:50
  115.7 10.4 %copy.19 = bf16[64,8,128,128]{3,2,1,0:T(8,128)(2,1)S(1)} copy(bf16[64,8,128,128]{3,1,2,0:T(8,128)(2,1)} %fusion.5) | data formatting | bytes 33554432
  126.1 11.8 %copy.17 = bf16[8,64,128,128]{3,1,2,0:T(8,128)(2,1)} copy(bf16[8,64,128,128]{3,2,1,0:T(8,128)(2,1)S(1)} %bitcast.28) | data formatting | bytes 33554432 | tf_op jit(solution)/shard_map/reshape | solution.py:56
  138.0 56.6 %all-gather.7.cloned.1.call-done = bf16[8192,1024]{1,0:T(8,128)(2,1)} async-done(((bf16[512,1024]{1,0:T(8,128)(2,1)}), bf16[8192,1024]{1,0:T(8,128)(2,1)}) %all-gather.7.cloned.1.call-update) | async-done | bytes 16777232 | tf_op jit(solution)/shard_map/all_gather | solution.py:60
  194.6 23.8 %fusion.8 = bf16[1024,1024]{1,0:T(8,128)(2,1)} fusion(bf16[8192,1024]{1,0:T(8,128)(2,1)} %all-gather.7.cloned.1.call-done, bf16[128,8,64,128]{3,2,1,0:T(8,128)(2,1)} %bitcast.29), kind=kOutput, calls=%fused_computation.7 | convolution fusion | flops 17180917760 | bytes 35651584 | tf_op jit(solution)/shard_map/dot_general | solution.py:58
  (14 shorter events, 0.8 us)
Async XLA Ops:
  6.5 90.7 %all-gather.9.cloned.1.call-start = ((), (), s32[]{:S(2)}) async-start(), calls=%async_computation.5 | async-start | bytes 9437184 | tf_op jit(solution)/shard_map/all_gather | solution.py:31
  31.1 163.5 %all-gather.7.cloned.1.call-start = ((), (), s32[]{:S(2)}) async-start(), calls=%async_computation.4 | async-start | bytes 17825792 | tf_op jit(solution)/shard_map/all_gather | solution.py:60
  33.2 10.0 %all-to-all-start.1 = ((s32[16,1,1]{2,1,0:T(1,128)}), s32[16,1,1]{2,1,0:T(1,128)S(1)}, u32[]{:S(2)}, u32[]{:S(2)}) async-start(s32[16,1,1]{2,1,0:T(1,128)} %copy.15), calls=%async_computation.1 | async-start | bytes 16384 | tf_op jit(solution)/shard_map/all_to_all | solution.py:28
  43.3 16.1 %all-to-all-start = ((s32[16,1,2]{2,1,0:T(1,128)}), s32[16,1,2]{2,1,0:T(1,128)S(1)}, u32[]{:S(2)}, u32[]{:S(2)}) async-start(s32[16,1,2]{2,1,0:T(1,128)} %copy.14), calls=%async_computation | async-start | bytes 16384 | tf_op jit(solution)/shard_map/all_to_all | solution.py:22
  59.4 23.2 %all-to-all-start.2 = ((s32[16,1,2]{2,1,0:T(1,128)}), s32[16,1,2]{2,1,0:T(1,128)S(1)}, u32[]{:S(2)}, u32[]{:S(2)}) async-start(s32[16,1,2]{2,1,0:T(1,128)} %copy.16), calls=%async_computation.2 | async-start | bytes 16384 | tf_op jit(solution)/shard_map/all_to_all | solution.py:25
Sparse Core Ops, SparseCore 0:
  31.3 49.8 all-gather.8
  83.3 111.2 all-gather.6
where the time goes:
time: 226 us; the launch traced here: 225 us
  blocking collectives  62.3 us (28%)
  waiting for transfers between devices  59.1 us (26%)
  matrix products  42.3 us (19%)
  local copies, waits for them, and re-layouts  28.9 us (13%)
  starting transfers between devices  15.5 us (7%)
  between operations  14.2 us (6%)
  other arithmetic  2.97 us (1%)
    all_gather x1, waiting for transfers between devices, body(): lax.all_gather(b_matrix, 'grid', axis=0, tiled=True)  56.6 us
    all_to_all x1, blocking collectives, body(): lax.all_to_all(a_slots.reshape(groups, CAP, block_size, block_size), 'gri...  24.6 us
    dot_general x1, matrix products, body(): jnp.dot(tile, lax.all_gather(b_matrix, 'grid', axis=0, tiled=True), prefe...  23.8 us
    dot_general x1, matrix products, body(): jnp.einsum('sp,sq->pq', placing, slot_data.reshape(total, block_size * bl...  18.5 us
    all_gather x1, blocking collectives, body(): lax.all_gather(landed[1][None], 'blk', axis=0, tiled=True)  14.7 us
    all_gather x1, blocking collectives, body(): lax.all_gather(landed[2][None], 'blk', axis=0, tiled=True)  12.8 us
    unnamed x4, local copies, waits for them, and re-layouts  11.9 us
    reshape x1, local copies, waits for them, and re-layouts, body(): spread.astype(jnp.bfloat16).reshape(RB, k_blocks, block_size, block_size)  11.8 us
  transfers between devices with their start and end apart: 5, of which 2 were waited for; matrix products, arithmetic and copies ran while one was open for 22% of the time, Pallas kernels for 0%

commit v1 on v0

v1 whole, which is shorter than its diff:
```python
import jax
import jax.numpy as jnp
from jax import lax
from jax.experimental import pallas as pl
from jax.experimental.pallas import tpu as pltpu
from jax.sharding import PartitionSpec as P

CAP = 2
RB = 8
BS = 128
NY = 4
NZ = 4
NX = 4
NK = 64
NSLOT = 256
MESH = pl.DeviceIdType.MESH
F32 = jnp.float32
BF16 = jnp.bfloat16

HALF = 256
SUB = 128


def wrap(v):
    return lax.rem(v + 4, 4)


def build_labels():
    names = []
    for h in (0, 1):
        for s in (1, -1):
            names += [("m1", h, s), ("m2", h, s)]
            for j in (0, -1, 1):
                names += [("m3", h, j, s), ("m4", h, j, s)]
            names += [("m3a", h, s), ("m3b", h, s), ("m4", h, 2, s)]
    return {n: i for i, n in enumerate(names)}


LABELS = build_labels()
XLABELS = {n: i for i, n in enumerate(
    [(t, s) for s in (1, -1) for t in ("first", "second", "fwd", "meta")]
)}
CLABELS = {n: i for i, n in enumerate(["own", "xp1", "xp2", "xm1", "xm2", "far1", "far2", "mown", "mp", "mm", "mf"])}


def kernel(a_ref, rows_ref, cols_ref, cnt_ref, owned_ref, b_ref, o_ref,
           bpan, slots, tile, acc, outb, mine, mland, msm, idxv, idxs,
           bs, br, xs, xr, cs, cr, a1s, a1r, ms, mr, loc, oloc):
    g = lax.axis_index("grid")
    b = lax.axis_index("blk")
    y, z = g // NZ, lax.rem(g, NZ)
    x, c = b // 2, lax.rem(b, 2)

    def gid(dy, dz):
        return wrap(y + dy) * NZ + wrap(z + dz)

    def bid(dx):
        return wrap(x + dx) * 2 + c

    sib = x * 2 + (1 - c)

    code = rows_ref[...] * NK + cols_ref[...]
    cap_at = lax.broadcasted_iota(jnp.int32, (CAP, 16), 0)
    code = jnp.where(cap_at < cnt_ref[...], code, -1)
    mine[...] = jnp.full((CAP, 128), -1, jnp.int32)
    mine[:, 0:16] = code

    bar = pltpu.get_barrier_semaphore()

    @pl.loop(1, 16)
    def _(j):
        q = lax.rem(g + j, 16)
        pl.semaphore_signal(bar, 1, device_id=(q, b), device_id_type=MESH)

    for other in (bid(1), bid(-1), sib):
        pl.semaphore_signal(bar, 1, device_id=(g, other), device_id_type=MESH)
    pl.semaphore_wait(bar, 18)

    def start(src, dst, ssem, rsem, dev):
        pltpu.make_async_remote_copy(
            src_ref=src, dst_ref=dst, send_sem=ssem, recv_sem=rsem,
            device_id=dev, device_id_type=MESH).start()

    def arrive(ref, sem):
        pltpu.make_async_copy(ref, ref, sem).wait()

    def at(h, f, s):
        return gid(f, s) if h == 0 else gid(s, f)

    def region(h, f, s, part):
        lo = h * HALF + (SUB if part == "b" else 0)
        n = HALF if part == "ab" else SUB
        return bpan.at[at(h, f, s), pl.ds(lo, n)]

    def send(label, h, f, s, part, df, ds, own=False):
        i = LABELS[label]
        dst = region(h, f, s, part)
        if own:
            lo = h * HALF + (SUB if part == "b" else 0)
            n = HALF if part == "ab" else SUB
            src = b_ref.at[pl.ds(lo, n)]
        else:
            src = dst
        start(src, dst, bs.at[i], br.at[i], (at(h, df, ds), b))

    def got(label, h, f, s, part):
        arrive(region(h, f, s, part), br.at[LABELS[label]])

    SUBOF = {1: "a", -1: "b"}

    @pl.loop(1, 16)
    def _(j):
        q = lax.rem(g + j, 16)
        start(mine, mland.at[b * 16 + g], ms, mr, (q, b))

    @pl.loop(1, 16)
    def _(j):
        q = lax.rem(g + j, 16)
        start(a_ref.at[pl.ds(q * CAP, CAP)], slots.at[pl.ds(b * 32 + g * CAP, CAP)], a1s, a1r, (q, b))

    for h in (0, 1):
        for s in (1, -1):
            send(("m1", h, s), h, 0, 0, "ab", s, 0, own=True)
    for h in (0, 1):
        for s in (1, -1):
            send(("m3", h, 0, s), h, 0, 0, "ab", 0, s, own=True)
    own_b = pltpu.make_async_copy(b_ref, bpan.at[g], loc.at[0])
    own_b.start()
    own_a = pltpu.make_async_copy(a_ref.at[pl.ds(g * CAP, CAP)], slots.at[pl.ds(b * 32 + g * CAP, CAP)], loc.at[1])
    own_a.start()
    own_m = pltpu.make_async_copy(mine, mland.at[b * 16 + g], loc.at[2])
    own_m.start()
    own_a.wait()
    own_m.wait()
    arrive(slots.at[pl.ds(0, 30)], a1r)
    arrive(mland.at[pl.ds(0, 15)], mr)

    def srow(bb, part):
        if part == "all":
            return slots.at[pl.ds(bb * 32, 32)]
        return slots.at[pl.ds(bb * 32 + (16 if part == "b" else 0), 16)]

    def mrow(bb):
        return mland.at[pl.ds(bb * 16, 16)]

    def xsend(label, ref, s):
        i = XLABELS[(label, s)]
        start(ref, ref, xs.at[i], xr.at[i], (g, bid(s)))

    def xgot(label, ref, s):
        arrive(ref, xr.at[XLABELS[(label, s)]])

    def csend(label, ref):
        i = CLABELS[label]
        start(ref, ref, cs.at[i], cr.at[i], (g, sib))

    def cgot(label, ref):
        arrive(ref, cr.at[CLABELS[label]])

    for s in (1, -1):
        xsend("meta", mrow(b), s)
        xsend("first", srow(b, "a" if s == 1 else "b"), s)
        xsend("second", srow(b, "b" if s == 1 else "a"), s)
    csend("own", srow(b, "all"))
    csend("mown", mrow(b))

    for h in (0, 1):
        for s in (1, -1):
            got(("m1", h, s), h, -s, 0, "ab")
            send(("m2", h, s), h, -s, 0, SUBOF[s], s, 0)
    for h in (0, 1):
        for j in (-1, 1):
            for s in (1, -1):
                send(("m3", h, j, s), h, j, 0, "ab", 0, s)

    for s in (1, -1):
        xgot("meta", mrow(bid(-s)), s)
        csend("mp" if s == 1 else "mm", mrow(bid(-s)))
        if s == 1:
            start(mrow(bid(-1)), mrow(bid(-1)), loc.at[3], loc.at[4], (g, bid(1)))
        xgot("first", srow(bid(-s), "a" if s == 1 else "b"), s)
        xsend("fwd", srow(bid(-s), "a" if s == 1 else "b"), s)
        csend("xp1" if s == 1 else "xm1", srow(bid(-s), "a" if s == 1 else "b"))

    for h in (0, 1):
        for s in (1, -1):
            got(("m3", h, 0, s), h, 0, -s, "ab")
            send(("m4", h, 0, s), h, 0, -s, SUBOF[s], 0, s)
    for h in (0, 1):
        got(("m2", h, 1), h, 2, 0, "a")
        for s in (1, -1):
            send(("m3a", h, s), h, 2, 0, "a", 0, s)
        got(("m2", h, -1), h, 2, 0, "b")
        for s in (1, -1):
            send(("m3b", h, s), h, 2, 0, "b", 0, s)

    for s in (1, -1):
        xgot("second", srow(bid(-s), "b" if s == 1 else "a"), s)
        csend("xp2" if s == 1 else "xm2", srow(bid(-s), "b" if s == 1 else "a"))
    arrive(mrow(bid(2)), loc.at[4])
    csend("mf", mrow(bid(2)))
    xgot("fwd", srow(bid(2), "a"), 1)
    csend("far1", srow(bid(2), "a"))
    xgot("fwd", srow(bid(2), "b"), -1)
    csend("far2", srow(bid(2), "b"))

    def sb(dx):
        return wrap(x + dx) * 2 + (1 - c)

    cgot("mown", mrow(sb(0)))
    cgot("mp", mrow(sb(-1)))
    cgot("mm", mrow(sb(1)))
    cgot("mf", mrow(sb(2)))

    meta_copy = pltpu.make_async_copy(mland, msm, loc.at[5])
    meta_copy.start()
    meta_copy.wait()
    sub_at = lax.broadcasted_iota(jnp.int32, (RB, 128), 0)
    lane_at = lax.broadcasted_iota(jnp.int32, (RB, 128), 1)
    want = lane_at
    for i in range(RB):
        want = jnp.where(sub_at == i, owned_ref[0, i] * NK + lane_at, want)
    want = jnp.where(lane_at < NK, want, -2)

    def find(r, where):
        for cap in range(CAP):
            where = jnp.where(want == msm[r, cap, g], r * CAP + cap, where)
        return where

    idxv[...] = lax.fori_loop(0, NSLOT // CAP, find, jnp.full((RB, 128), -1, jnp.int32))
    idx_copy = pltpu.make_async_copy(idxv, idxs, loc.at[6])
    idx_copy.start()
    idx_copy.wait()

    cgot("own", srow(sb(0), "all"))
    cgot("xp1", srow(sb(-1), "a"))
    cgot("xm1", srow(sb(1), "b"))
    cgot("xp2", srow(sb(-1), "b"))
    cgot("xm2", srow(sb(1), "a"))
    cgot("far1", srow(sb(2), "a"))
    cgot("far2", srow(sb(2), "b"))

    @pl.loop(0, 16)
    def _(p):
        for kk in range(4):
            for i in range(RB):
                s = idxs[i, p * 4 + kk]
                data = slots[jnp.maximum(s, 0)]
                tile[p, i * BS:(i + 1) * BS, kk * BS:(kk + 1) * BS] = jnp.where(s >= 0, data, jnp.zeros_like(data))

    def mm(p, lo, n, first=False):
        @pl.loop(0, 4)
        def _(t):
            col = pl.ds(pl.multiple_of(t * 256, 256), 256)
            part = jnp.dot(tile[p, :, lo:lo + n], bpan[p, lo:lo + n, col], preferred_element_type=F32)
            if first:
                acc[:, col] = part
            else:
                acc[:, col] += part

    own_b.wait()
    mm(gid(0, 0), 0, 512, first=True)
    for h, j in ((0, -1), (1, -1), (0, 1), (1, 1)):
        mm(at(h, j, 0), 0, 512)

    for h in (0, 1):
        for j in (-1, 1):
            for s in (1, -1):
                got(("m3", h, j, s), h, j, -s, "ab")
                send(("m4", h, j, s), h, j, -s, SUBOF[s], 0, s)
    for dy in (-1, 1):
        for dz in (-1, 1):
            mm(gid(dy, dz), 0, 512)

    for h in (0, 1):
        for s in (1, -1):
            got(("m3a", h, s), h, 2, -s, "a")
            got(("m3b", h, s), h, 2, -s, "b")
            send(("m4", h, 2, s), h, 2, -s, SUBOF[s], 0, s)
    for h in (0, 1):
        got(("m4", h, 0, 1), h, 0, 2, "a")
        got(("m4", h, 0, -1), h, 0, 2, "b")
    mm(gid(2, 0), 0, 512)
    mm(gid(0, 2), 0, 512)
    for h in (0, 1):
        for j in (-1, 1):
            got(("m4", h, j, 1), h, j, 2, "a")
            got(("m4", h, j, -1), h, j, 2, "b")
    for d in (-1, 1):
        mm(gid(2, d), 0, 512)
        mm(gid(d, 2), 0, 512)
    for h in (0, 1):
        got(("m4", h, 2, 1), h, 2, 2, "a")
        got(("m4", h, 2, -1), h, 2, 2, "b")

    last = gid(2, 2)
    for t in range(4):
        col = pl.ds(t * 256, 256)
        part = jnp.dot(tile[last], bpan[last, :, col], preferred_element_type=F32)
        outb[:, col] = (acc[:, col] + part).astype(BF16)
        pltpu.make_async_copy(outb.at[:, col], o_ref.at[:, col], oloc.at[t]).start()
    for t in range(4):
        col = pl.ds(t * 256, 256)
        pltpu.make_async_copy(outb.at[:, col], o_ref.at[:, col], oloc.at[t]).wait()

    arrive(slots.at[pl.ds(0, 30)], a1s)
    arrive(mland.at[pl.ds(0, 15)], ms)
    arrive(mrow(b), loc.at[3])
    for name, i in LABELS.items():
        n = HALF if name[0] in ("m1", "m3") else SUB
        arrive(bpan.at[0, pl.ds(0, n)], bs.at[i])
    for (t, s), i in XLABELS.items():
        arrive(mrow(b) if t == "meta" else srow(b, "a"), xs.at[i])
    for t, i in CLABELS.items():
        arrive(mrow(b) if t[0] == "m" else srow(b, "all" if t == "own" else "a"), cs.at[i])


def body(a_slots, a_rows, a_cols, a_count, owned_rows, b_matrix):
    DMA = pltpu.SemaphoreType.DMA
    any_space = pl.BlockSpec(memory_space=pl.ANY)
    vmem = pl.BlockSpec(memory_space=pltpu.VMEM)
    smem = pl.BlockSpec(memory_space=pltpu.SMEM)
    return pl.pallas_call(
        kernel,
        out_shape=jax.ShapeDtypeStruct((RB * BS, b_matrix.shape[1]), BF16),
        in_specs=[any_space, vmem, vmem, vmem, smem, any_space],
        out_specs=any_space,
        scratch_shapes=[
            pltpu.VMEM((16, 512, 1024), BF16),
            pltpu.VMEM((NSLOT, BS, BS), BF16),
            pltpu.VMEM((16, RB * BS, 512), BF16),
            pltpu.VMEM((RB * BS, 1024), F32),
            pltpu.VMEM((RB * BS, 1024), BF16),
            pltpu.VMEM((CAP, 128), jnp.int32),
            pltpu.VMEM((128, CAP, 128), jnp.int32),
            pltpu.SMEM((128, CAP, 128), jnp.int32),
            pltpu.VMEM((RB, 128), jnp.int32),
            pltpu.SMEM((RB, 128), jnp.int32),
            DMA((len(LABELS),)), DMA((len(LABELS),)),
            DMA((len(XLABELS),)), DMA((len(XLABELS),)),
            DMA((len(CLABELS),)), DMA((len(CLABELS),)),
            DMA, DMA, DMA, DMA, DMA((7,)), DMA((4,)),
        ],
        compiler_params=pltpu.CompilerParams(
            collective_id=0, has_side_effects=True, vmem_limit_bytes=60 << 20),
    )(
        a_slots.reshape(16 * CAP, BS, BS),
        a_rows.reshape(16, CAP).T,
        a_cols.reshape(16, CAP).T,
        a_count.reshape(1, 16),
        owned_rows,
        b_matrix,
    )


def solution(mesh):
    in_specs = (
        P("grid", "blk", None, None, None, None),
        P("grid", "blk", None, None),
        P("grid", "blk", None, None),
        P("grid", "blk", None),
        P("grid", None),
        P("grid", "blk"),
    )
    return jax.shard_map(body, mesh=mesh, in_specs=in_specs, out_specs=P("grid", "blk"), check_vma=False)
```

time: 226 us -> 115 us (0.51)
  Pallas kernels: 0 us -> 111 us
  blocking collectives: 62.3 us -> 0 us
  waiting for transfers between devices: 59.1 us -> 0 us
  matrix products: 42.3 us -> 0 us
  local copies, waits for them, and re-layouts: 28.9 us -> 3.08 us
  starting transfers between devices: 15.5 us -> 0 us
  between operations: 14.2 us -> 0.01 us
  other arithmetic: 2.97 us -> 0 us
    pallas_call x0 -> x1, Pallas kernels: none -> 111 us  [body(): pl.pallas_call(kernel, out_shape=jax.ShapeDtypeStruct((RB * BS, b_matrix....]
    all_gather x2 -> x0, waiting for transfers between devices: 56.6 us -> none  [the longest x1 56.6 us: body(): lax.all_gather(b_matrix, 'grid', axis=0, tiled=True)]
    dot_general x2 -> x0, matrix products: 42.3 us -> none  [the longest x1 23.8 us: body(): jnp.dot(tile, lax.all_gather(b_matrix, 'grid', axis=0, tiled=True), prefe...]
    all_gather x2 -> x0, blocking collectives: 27.4 us -> none  [the longest x1 14.7 us: body(): lax.all_gather(landed[1][None], 'blk', axis=0, tiled=True)]
    all_to_all x1 -> x0, blocking collectives: 24.6 us -> none  [body(): lax.all_to_all(a_slots.reshape(groups, CAP, block_size, block_size), 'gri...]
    all_to_all x3 -> x0, starting transfers between devices: 15.4 us -> none  [the longest x1 6.94 us: body(): lax.all_to_all(a_cols.reshape(groups, CAP), 'grid', split_axis=0, concat_...]
    reshape x1 -> x0, local copies, waits for them, and re-layouts: 11.8 us -> none  [body(): spread.astype(jnp.bfloat16).reshape(RB, k_blocks, block_size, block_size)]
    unnamed x1 -> x0, blocking collectives: 10.3 us -> none
  transfers between devices with their start and end apart: 5 -> 0, of which waited for: 2 -> 0; matrix products, arithmetic and copies ran while one was open for 22% -> 0% of each run, Pallas kernels for 0% -> 0%
where the time goes in v1:
time: 115 us; the launch traced here: 114 us
  Pallas kernels  111 us (97%)
  local copies, waits for them, and re-layouts  3.08 us (3%)
    pallas_call x1, Pallas kernels, body(): pl.pallas_call(kernel, out_shape=jax.ShapeDtypeStruct((RB * BS, b_matrix....  111 us
    unnamed x1, local copies, waits for them, and re-layouts  3.08 us

profile of v1, /device:TPU:1, one launch (start us, length us, event | category | flops | bytes accessed | tf_op | source)
XLA Modules:
  0.0 113.7 jit_solution(8013235496631359812)
XLA Ops:
  0.0 110.6 %shard_map.64 = bf16[1024,1024]{1,0:T(8,128)(2,1)} custom-call(bf16[32,128,128]{2,1,0:T(8,128)(2,1)} %bitcast.8, s32[2,16]{1,0:T(2,128)} %bitcast.9, s32[2,16]{1,0:T(2,128)} %bitcast.10, s32[1,16]{1,0:T(1,128)} %bitcast.11, s32[1,8]{1,0:T(1,128)} %owned_ref.1, bf16[512,1024]{1,0:T(8,128)(2,1)} %b_ref.1), custom_call_target="tpu_custom_call" | custom-call | tf_op jit(solution)/shard_map/pallas_call | solution.py:323
  110.6 3.1 %copy.8 = bf16[1024,1024]{1,0:T(8,128)(2,1)} copy(bf16[1024,1024]{1,0:T(8,128)(2,1)} %shard_map.64) | data formatting | bytes 4194304

commit v2 on v0

v2 whole, which is shorter than its diff:
```python
import jax
import jax.numpy as jnp
from jax import lax
from jax.experimental import pallas as pl
from jax.experimental.pallas import tpu as pltpu
from jax.sharding import PartitionSpec as P

CAP = 2
RB = 8
BS = 128
NZ = 4
NK = 64
WIDTH = (256, 256)
LEFT = (0, 256)
CH = 16
SF = 12
R1 = 288
ROWS = 512
NONE = 256
PIECES = ((0, 0), (0, 1), (0, 3), (1, 0), (0, 2), (1, 1), (1, 3), (1, 2))
MESH = pl.DeviceIdType.MESH
F32 = jnp.float32
BF16 = jnp.bfloat16


def wrap(v):
    return lax.rem(v + 4, 4)


class Labels:
    def __init__(self, names):
        self.at = {n: i for i, n in enumerate(names)}

    def __len__(self):
        return len(self.at)


B_LABELS = Labels(
    [(n, k) for n in (0, 1) for k in ("cross", "w1", "w2own", "w2a", "w2b")]
    + [(n, k, s) for n in (0, 1) for s in (1, -1)
       for k in ("z1own", "z1far", "z2own", "z2far", "y1own", "y2own", "w2")]
)
X_LABELS = Labels(
    [(k, i, t, s) for k in (0, 1) for i in "OQ" for t in ("full", "fwd") for s in (1, -1)
     if (k, i, t) not in ((0, "O", "full"), (1, "O", "full"))]
    + [(1, "O", t, s) for t in ("fulla", "fullb") for s in (1, -1)]
    + [("piece", j, s) for j in range(8) for s in (1, -1)]
    + [("meta", 1), ("meta", -1), ("metafwd", 1)]
)
P_LABELS = Labels([("pa", k) for k in (0, 1)] + [("pf", d) for d in (0, 1, -1, 2)])
C_LABELS = Labels(
    [(k, i, t) for k in (0, 1) for i in "OQ" for t in ("own", "xp", "xm", "fp", "fm")]
    + [("pf", d) for d in (0, 1, -1, 2)]
    + ["m0", "mp", "mm", "mf"]
)


def kernel(a_ref, rows_ref, cols_ref, cnt_ref, owned_ref, b_ref, o_ref,
           bp0, bp1, bx0, bx1, slots0, slots1, accp0, accp1, acco0, acco1, outp0, outp1, mine, mland, msm, idxv, idxs,
           bs, br, xs, xr, ps, pr, cs, cr, a1s, a1r, ms, mr, loc, outs, outr):
    g = lax.axis_index("grid")
    b = lax.axis_index("blk")
    y, z = g // NZ, lax.rem(g, NZ)
    x, c = b // 2, lax.rem(b, 2)

    def side(yv):
        return lax.rem((yv + 1) // 2, 2)

    def partner(yv):
        return yv + 1 - 2 * lax.rem(yv, 2)

    def order(yv, zv):
        return side(yv) * 8 + (yv // 2) * 4 + zv

    s = side(y)
    t = 1 - s
    gp = partner(y) * NZ + z
    gcls = (gp, g)
    pair = (gp, b)
    across = ((3 - y) * NZ + z, b)
    sib = x * 2 + (1 - c)

    def bid(dx):
        return wrap(x + dx) * 2 + c

    def sb(dx):
        return wrap(x + dx) * 2 + (1 - c)

    def zdev(d):
        return (y * NZ + wrap(z + d), b)

    slots = (slots0, slots1)
    bp, bx, outp = (bp0, bp1), (bx0, bx1), (outp0, outp1)
    accs = ((accp0, accp1), (acco0, acco1))

    code = rows_ref[...] * NK + cols_ref[...]
    cap_at = lax.broadcasted_iota(jnp.int32, (CAP, 16), 0)
    code = jnp.where(cap_at < cnt_ref[...], code, -1)
    mine[...] = jnp.full((1, 128), -1, jnp.int32)
    for cap in range(CAP):
        mine[:, cap * 16:cap * 16 + 16] = code[cap:cap + 1]
    mine[:, 32:32 + RB] = owned_ref[...]
    for k in (0, 1):
        slots[k][NONE] = jnp.zeros((BS, BS), BF16)

    bar = pltpu.get_barrier_semaphore()

    @pl.loop(1, 16)
    def _(j):
        q = lax.rem(g + j, 16)
        pl.semaphore_signal(bar, 1, device_id=(q, b), device_id_type=MESH)

    for other in (bid(1), bid(-1), sib):
        pl.semaphore_signal(bar, 1, device_id=(g, other), device_id_type=MESH)
    pl.semaphore_wait(bar, 18)

    def start(src, dst, ssem, rsem, dev):
        pltpu.make_async_remote_copy(
            src_ref=src, dst_ref=dst, send_sem=ssem, recv_sem=rsem,
            device_id=dev, device_id_type=MESH).start()

    def arrive(ref, sem):
        pltpu.make_async_copy(ref, ref, sem).wait()

    def k0(yv, zv):
        return (yv // 2) * 8 + zv * 2

    def breg(n, yv, zv, part):
        lo, cnt = {
            "w": (0, R1), "wa": (0, R1 // 2), "wb": (R1 // 2, R1 // 2),
            "z": (R1, ROWS - R1), "za": (R1, (ROWS - R1) // 2),
            "zb": (R1 + (ROWS - R1) // 2, (ROWS - R1) // 2),
        }[part]
        return bp[n].at[pl.ds(k0(yv, zv), 2), pl.ds(lo, cnt)]

    def chunk(k, b0, s0, lo=0, n=CH):
        return slots[k].at[pl.ds(b0 * 32 + s0 * CH + lo, n)]

    def bsend(label, ref, dev):
        i = B_LABELS.at[label]
        start(ref, ref, bs.at[i], br.at[i], dev)

    def bgot(label, ref):
        arrive(ref, br.at[B_LABELS.at[label]])

    def xsend(label, ref, d):
        i = X_LABELS.at[label]
        start(ref, ref, xs.at[i], xr.at[i], (g, bid(d)))

    def xgot(label, ref):
        arrive(ref, xr.at[X_LABELS.at[label]])

    def psend(label, k, *where):
        i = P_LABELS.at[label]
        start(chunk(k, *where), chunk(1 - k, *where), ps.at[i], pr.at[i], pair)

    def pgot(label, ref):
        arrive(ref, pr.at[P_LABELS.at[label]])

    def csend(label, ref):
        i = C_LABELS.at[label]
        start(ref, ref, cs.at[i], cr.at[i], (g, sib))

    def cgot(label, ref):
        arrive(ref, cr.at[C_LABELS.at[label]])

    here = order(y, z) * CAP

    def a_dst(k):
        return slots[k].at[pl.ds(b * 32 + here, CAP)]

    def a_send(k):
        for j, (far, dz) in enumerate(PIECES):
            yv, zv = (3 - y if far else y), wrap(z + dz)
            owner = (partner(yv) if k == 0 else yv) * NZ + zv
            src = a_ref.at[pl.ds(owner * CAP, CAP)]
            rsem = a1r.at[j] if k == 0 else a1r.at[8]
            if j == 0:
                pltpu.make_async_copy(src, a_dst(k), loc.at[6 + k]).start()
            else:
                start(src, a_dst(k), a1s.at[k], rsem, (yv * NZ + zv, b))

    def piece(j, b0):
        far, dz = PIECES[j]
        at = order(3 - y if far else y, wrap(z - dz)) * CAP
        return slots0.at[pl.ds(b0 * 32 + at, CAP)]

    def x_pieces(js):
        for j in js:
            arrive(piece(j, b), loc.at[6] if j == 0 else a1r.at[j])
            for d in (1, -1):
                xsend(("piece", j, d), piece(j, b), d)

    kown = k0(y, z) + lax.rem(y, 2)

    def b_cols(side_at, n):
        return pl.ds(pl.multiple_of(side_at * 512 + LEFT[n], 128), WIDTH[n])

    a_send(0)
    own_b, cross_b = [], []
    for n in (0, 1):
        cp = pltpu.make_async_copy(b_ref.at[:, b_cols(t, n)], bx[n], loc.at[n])
        cp.start()
        cross_b.append(cp)
    for n in (0, 1):
        cp = pltpu.make_async_copy(b_ref.at[:, b_cols(s, n)], bp[n].at[kown], loc.at[2 + n])
        cp.start()
        own_b.append(cp)
    for n in (0, 1):
        cross_b[n].wait()
        i = B_LABELS.at[(n, "cross")]
        start(bx[n], bp[n].at[kown], bs.at[i], br.at[i], pair)

    @pl.loop(1, 16)
    def _(j):
        q = lax.rem(g + j, 16)
        start(mine, mland.at[b * 16 + g], ms, mr, (q, b))

    pltpu.make_async_copy(mine, mland.at[b * 16 + g], loc.at[8]).start()

    kpair = k0(y, z) + 1 - lax.rem(y, 2)

    def b_start(n):
        own_b[n].wait()
        bgot((n, "cross"), bp[n].at[kpair])
        bsend((n, "w1"), breg(n, y, z, "w"), across)
        for d in (1, -1):
            bsend((n, "z1own", d), breg(n, y, z, "w"), zdev(d))
        for d in (1, -1):
            bsend((n, "y1own", d), breg(n, y, z, "z"), zdev(d))
        bsend((n, "w2own"), breg(n, y, z, "z"), across)

    HALF = {1: "a", -1: "b"}

    def b_step1(n):
        bgot((n, "w1"), breg(n, 3 - y, z, "w"))
        for d in (1, -1):
            bsend((n, "z1far", d), breg(n, 3 - y, z, "w"), zdev(d))
        for d in (1, -1):
            bgot((n, "z1own", d), breg(n, y, wrap(z - d), "w"))
            bsend((n, "z2own", d), breg(n, y, wrap(z - d), "w" + HALF[d]), zdev(d))

    def b_step2(n):
        for d in (1, -1):
            bgot((n, "y1own", d), breg(n, y, wrap(z - d), "z"))
            bsend((n, "w2", d), breg(n, y, wrap(z - d), "z"), across)
            bsend((n, "y2own", d), breg(n, y, wrap(z - d), "z" + HALF[d]), zdev(d))

    def b_step3(n):
        for d in (1, -1):
            bgot((n, "z1far", d), breg(n, 3 - y, wrap(z - d), "w"))
            bsend((n, "z2far", d), breg(n, 3 - y, wrap(z - d), "w" + HALF[d]), zdev(d))
        for d in (1, -1):
            bgot((n, "y2own", d), breg(n, y, wrap(z + 2), "z" + HALF[d]))
            bsend((n, "w2" + HALF[d]), breg(n, y, wrap(z + 2), "z" + HALF[d]), across)

    def b_got_q(n, q):
        if q == 0:
            bgot((n, "w2own"), breg(n, 3 - y, z, "z"))
        elif q < 3:
            d = -1 if q == 1 else 1
            bgot((n, "w2", d), breg(n, 3 - y, wrap(z - d), "z"))
        else:
            for d in (1, -1):
                bgot((n, "z2own", d), breg(n, y, wrap(z + 2), "w" + HALF[d]))
                bgot((n, "z2far", d), breg(n, 3 - y, wrap(z + 2), "w" + HALF[d]))
                bgot((n, "w2" + HALF[d]), breg(n, 3 - y, wrap(z + 2), "z" + HALF[d]))

    def item(k, i, b0, part="all"):
        s0, n = (s, CH) if i == "O" else (t, SF if k == 1 else CH)
        h = n // 2
        lo, cnt = {"all": (0, n), "a": (0, h), "b": (h, n - h)}[part]
        return chunk(k, b0, s0, lo, cnt)

    def x_full(k, i):
        for d in (1, -1):
            xsend((k, i, "full", d), item(k, i, b), d)
        csend((k, i, "own"), item(k, i, b))

    def x_part(part):
        for d in (1, -1):
            xsend((1, "O", "full" + part, d), item(1, "O", b, part), d)

    def x_fwd(k, i):
        for d in (1, -1):
            if (k, i) == (0, "O"):
                for j in range(8):
                    xgot(("piece", j, d), piece(j, bid(-d)))
            elif (k, i) == (1, "O"):
                for part in "ab":
                    xgot((k, i, "full" + part, d), item(k, i, bid(-d), part))
            else:
                xgot((k, i, "full", d), item(k, i, bid(-d)))
            xsend((k, i, "fwd", d), item(k, i, bid(-d), HALF[d]), d)
            csend((k, i, "xp" if d == 1 else "xm"), item(k, i, bid(-d)))

    def x_last(k, i):
        for d in (1, -1):
            xgot((k, i, "fwd", d), item(k, i, bid(2), HALF[d]))
            csend((k, i, "fp" if d == 1 else "fm"), item(k, i, bid(2), HALF[d]))

    def c_end(k, i):
        cgot((k, i, "own"), item(k, i, sb(0)))
        cgot((k, i, "xp"), item(k, i, sb(-1)))
        cgot((k, i, "xm"), item(k, i, sb(1)))
        cgot((k, i, "fp"), item(k, i, sb(2), "a"))
        cgot((k, i, "fm"), item(k, i, sb(2), "b"))

    def p_rest():
        for d in (0, 1, -1, 2):
            psend(("pf", d), 0, bid(d), s, SF, CH - SF)

    def p_rest_got():
        for d in (0, 1, -1, 2):
            ref = chunk(1, bid(d), t, SF, CH - SF)
            pgot(("pf", d), ref)
            csend(("pf", d), ref)

    def c_rest_end():
        for d in (0, 1, -1, 2):
            cgot(("pf", d), chunk(1, sb(d), t, SF, CH - SF))

    def mrow(bb):
        return mland.at[pl.ds(bb * 16, 16)]

    def meta_start():
        pltpu.make_async_copy(mland, msm, loc.at[4]).start()

    def find_all():
        pltpu.make_async_copy(mland, msm, loc.at[4]).wait()
        sub_at = lax.broadcasted_iota(jnp.int32, (RB, 128), 0)
        lane_at = lax.broadcasted_iota(jnp.int32, (RB, 128), 1)
        wants = []
        for k in (0, 1):
            want = lane_at
            for i in range(RB):
                want = jnp.where(sub_at == i, msm[b * 16 + gcls[k], 0, 32 + i] * NK + lane_at, want)
            wants.append(jnp.where(lane_at < NK, want, -2))

        def find(b0, where):
            out = []
            for k in (0, 1):
                w = where[k]
                base = b0 * 32
                for g0 in range(16):
                    yv, zv = g0 // NZ, g0 % NZ
                    at = (((yv + 1) // 2) % 2 * 8 + (yv // 2) * 4 + zv) * CAP
                    for cap in range(CAP):
                        w = jnp.where(wants[k] == msm[b0 * 16 + g0, 0, cap * 16 + gcls[k]], base + at + cap, w)
                out.append(w)
            return tuple(out)

        none = jnp.full((RB, 128), NONE, jnp.int32)
        found = lax.fori_loop(0, 8, find, (none, none))
        for k in (0, 1):
            idxv[k] = found[k]
        idx_copy = pltpu.make_async_copy(idxv, idxs, loc.at[5])
        idx_copy.start()
        idx_copy.wait()

    DZ = (0, 1, -1, 2)

    def dot(k, n, q, rows=(0, RB)):
        zv = wrap(z + DZ[q])
        kbs = [k0(y, zv), k0(y, zv) + 1, k0(3 - y, zv), k0(3 - y, zv) + 1]
        lhs = []
        for i in range(*rows):
            blocks = []
            for kb in kbs:
                gb = ((kb // 8) * 2 + lax.rem(kb, 2)) * NZ + lax.rem(kb, 8) // 2
                blocks += [slots[k][idxs[k, i, gb * 4 + kk]] for kk in range(4)]
            lhs.append(jnp.concatenate(blocks, axis=1))
        rhs = jnp.concatenate(
            [bp[n][pl.ds(kb, 2)].reshape(2 * ROWS, WIDTH[n]) for kb in (kbs[0], kbs[2])], axis=0)
        return jnp.dot(jnp.concatenate(lhs, axis=0), rhs, preferred_element_type=F32)

    def add(k, n, q, rows=(0, RB)):
        lo, hi = rows[0] * BS, rows[1] * BS
        part = dot(k, n, q, rows)
        acc = accs[k][n]
        if q == 0:
            acc[lo:hi] = part
        elif q < 3:
            acc[lo:hi] += part
        elif k == 0:
            outp[n][lo:hi] = (acc[lo:hi] + part).astype(BF16)
        else:
            o_ref[lo:hi, b_cols(s, n)] = (acc[lo:hi] + part).astype(BF16)

    SWAPS = ((0, 0, 8), (1, 0, 4), (1, 4, 8))

    def swap(j):
        n, lo, hi = SWAPS[j]
        add(0, n, 3, (lo, hi))
        rows = pl.ds(lo * BS, (hi - lo) * BS)
        start(outp[n].at[rows], o_ref.at[rows, b_cols(s, n)], outs.at[j], outr.at[j], pair)

    x_pieces((0, 1, 2, 3))
    a_send(1)
    x_pieces((4, 5, 6, 7))
    csend((0, "O", "own"), item(0, "O", b))
    b_start(0)
    arrive(a_dst(1), loc.at[7])
    arrive(slots1.at[pl.ds(0, 14)], a1r.at[8])
    for k in (1, 0):
        psend(("pa", k), k, b, s, 0, SF if k == 0 else CH)
    csend((1, "O", "own"), item(1, "O", b))
    x_fwd(0, "O")
    x_part("a")
    arrive(mland.at[b * 16 + g], loc.at[8])
    arrive(mland.at[pl.ds(0, 15)], mr)
    for d in (1, -1):
        xsend(("meta", d), mrow(b), d)
    csend("m0", mrow(b))
    b_step1(0)
    x_last(0, "O")
    p_rest()
    pgot(("pa", 1), item(0, "Q", b))
    x_full(0, "Q")
    b_step2(0)
    b_start(1)
    for d in (1, -1):
        xgot(("meta", d), mrow(bid(-d)))
        csend("mp" if d == 1 else "mm", mrow(bid(-d)))
    xsend(("metafwd", 1), mrow(bid(-1)), 1)
    b_step3(0)
    x_fwd(0, "Q")
    x_part("b")
    xgot(("metafwd", 1), mrow(bid(2)))
    csend("mf", mrow(bid(2)))
    cgot("m0", mrow(sb(0)))
    cgot("mp", mrow(sb(-1)))
    cgot("mm", mrow(sb(1)))
    cgot("mf", mrow(sb(2)))
    meta_start()
    pgot(("pa", 0), item(1, "Q", b))
    x_full(1, "Q")
    find_all()
    x_last(0, "Q")
    for i in "OQ":
        c_end(0, i)
    b_got_q(0, 0)
    add(0, 0, 0)
    b_got_q(0, 1)
    add(0, 0, 1)
    b_step1(1)
    b_got_q(0, 2)
    add(0, 0, 2)
    b_got_q(0, 3)
    swap(0)
    x_fwd(1, "O")
    b_step2(1)
    p_rest_got()
    x_fwd(1, "Q")
    x_last(1, "O")
    b_step3(1)
    for q in range(3):
        b_got_q(1, q)
        add(0, 1, q)
    x_last(1, "Q")
    b_got_q(1, 3)
    swap(1)
    swap(2)
    for i in "OQ":
        c_end(1, i)
    c_rest_end()
    for n in (0, 1):
        for q in range(4):
            add(1, n, q)

    for j, (n, lo, hi) in enumerate(SWAPS):
        arrive(o_ref.at[pl.ds(lo * BS, (hi - lo) * BS), b_cols(t, n)], outr.at[j])

    for k in (0, 1):
        arrive(slots[k].at[pl.ds(0, 14)], a1s.at[k])
    arrive(mland.at[pl.ds(0, 15)], ms)
    sizes = {"cross": "x", "w1": "w", "z1own": "w", "z1far": "w", "z2own": "wa", "z2far": "wa",
             "y1own": "z", "y2own": "za", "w2own": "z", "w2": "z", "w2a": "za", "w2b": "zb"}
    for name, i in B_LABELS.at.items():
        part = sizes[name[1]]
        arrive(bx[name[0]] if part == "x" else breg(name[0], 0, 0, part), bs.at[i])
    for name, i in X_LABELS.at.items():
        if name[0] in ("meta", "metafwd"):
            arrive(mrow(b), xs.at[i])
        elif name[0] == "piece":
            arrive(piece(0, b), xs.at[i])
        else:
            k, it, kind, d = name
            arrive(item(k, it, b, {"full": "all", "fwd": HALF[d]}.get(kind, kind[-1])), xs.at[i])
    for name, i in P_LABELS.at.items():
        arrive(chunk(0, 0, 0, 0, {("pa", 0): SF, ("pa", 1): CH}.get(name, CH - SF)), ps.at[i])
    for name, i in C_LABELS.at.items():
        if isinstance(name, str):
            arrive(mrow(b), cs.at[i])
        elif name[0] == "pf":
            arrive(chunk(0, 0, 0, 0, CH - SF), cs.at[i])
        else:
            part = {"own": "all", "xp": "all", "xm": "all", "fp": "a", "fm": "b"}[name[2]]
            arrive(item(name[0], name[1], b, part), cs.at[i])
    for j, (n, lo, hi) in enumerate(SWAPS):
        arrive(outp[n].at[pl.ds(lo * BS, (hi - lo) * BS)], outs.at[j])


def body(a_slots, a_rows, a_cols, a_count, owned_rows, b_matrix):
    DMA = pltpu.SemaphoreType.DMA
    any_space = pl.BlockSpec(memory_space=pl.ANY)
    vmem = pl.BlockSpec(memory_space=pltpu.VMEM)
    return pl.pallas_call(
        kernel,
        out_shape=pltpu.VMEM((RB * BS, b_matrix.shape[1]), BF16),
        in_specs=[any_space, vmem, vmem, vmem, vmem, any_space],
        out_specs=vmem,
        scratch_shapes=[
            *[pltpu.VMEM((16, ROWS, w), BF16) for w in WIDTH],
            *[pltpu.VMEM((ROWS, w), BF16) for w in WIDTH],
            pltpu.VMEM((NONE + 1, BS, BS), BF16),
            pltpu.VMEM((NONE + 1, BS, BS), BF16),
            *[pltpu.VMEM((RB * BS, w), F32) for w in WIDTH * 2],
            *[pltpu.VMEM((RB * BS, w), BF16) for w in WIDTH],
            pltpu.VMEM((1, 128), jnp.int32),
            pltpu.VMEM((128, 1, 128), jnp.int32),
            pltpu.SMEM((128, 1, 128), jnp.int32),
            pltpu.VMEM((2, RB, 128), jnp.int32),
            pltpu.SMEM((2, RB, 128), jnp.int32),
            DMA((len(B_LABELS),)), DMA((len(B_LABELS),)),
            DMA((len(X_LABELS),)), DMA((len(X_LABELS),)),
            DMA((len(P_LABELS),)), DMA((len(P_LABELS),)),
            DMA((len(C_LABELS),)), DMA((len(C_LABELS),)),
            DMA((2,)), DMA((9,)), DMA, DMA, DMA((9,)), DMA((3,)), DMA((3,)),
        ],
        compiler_params=pltpu.CompilerParams(
            collective_id=0, has_side_effects=True, vmem_limit_bytes=60 << 20),
    )(
        a_slots.reshape(16 * CAP, BS, BS),
        a_rows.reshape(16, CAP).T,
        a_cols.reshape(16, CAP).T,
        a_count.reshape(1, 16),
        owned_rows,
        b_matrix,
    )


def solution(mesh):
    in_specs = (
        P("grid", "blk", None, None, None, None),
        P("grid", "blk", None, None),
        P("grid", "blk", None, None),
        P("grid", "blk", None),
        P("grid", None),
        P("grid", "blk"),
    )
    return jax.shard_map(body, mesh=mesh, in_specs=in_specs, out_specs=P("grid", "blk"), check_vma=False)
```

time: 226 us -> 102 us (0.45)
  Pallas kernels: 0 us -> 100 us
  blocking collectives: 62.3 us -> 0 us
  waiting for transfers between devices: 59.1 us -> 0 us
  matrix products: 42.3 us -> 0 us
  local copies, waits for them, and re-layouts: 28.9 us -> 1.32 us
  starting transfers between devices: 15.5 us -> 0 us
  between operations: 14.2 us -> 0.01 us
  other arithmetic: 2.97 us -> 0 us
    pallas_call x0 -> x1, Pallas kernels: none -> 100 us  [body(): pl.pallas_call(kernel, out_shape=pltpu.VMEM((RB * BS, b_matrix.shape[1]),...]
    all_gather x2 -> x0, waiting for transfers between devices: 56.6 us -> none  [the longest x1 56.6 us: body(): lax.all_gather(b_matrix, 'grid', axis=0, tiled=True)]
    dot_general x2 -> x0, matrix products: 42.3 us -> none  [the longest x1 23.8 us: body(): jnp.dot(tile, lax.all_gather(b_matrix, 'grid', axis=0, tiled=True), prefe...]
    all_gather x2 -> x0, blocking collectives: 27.4 us -> none  [the longest x1 14.7 us: body(): lax.all_gather(landed[1][None], 'blk', axis=0, tiled=True)]
    all_to_all x1 -> x0, blocking collectives: 24.6 us -> none  [body(): lax.all_to_all(a_slots.reshape(groups, CAP, block_size, block_size), 'gri...]
    all_to_all x3 -> x0, starting transfers between devices: 15.4 us -> none  [the longest x1 6.94 us: body(): lax.all_to_all(a_cols.reshape(groups, CAP), 'grid', split_axis=0, concat_...]
    reshape x1 -> x0, local copies, waits for them, and re-layouts: 11.8 us -> none  [body(): spread.astype(jnp.bfloat16).reshape(RB, k_blocks, block_size, block_size)]
    unnamed x4 -> x1, local copies, waits for them, and re-layouts: 11.9 us -> 1.32 us
  transfers between devices with their start and end apart: 5 -> 0, of which waited for: 2 -> 0; matrix products, arithmetic and copies ran while one was open for 22% -> 0% of each run, Pallas kernels for 0% -> 0%
where the time goes in v2:
time: 102 us
  Pallas kernels  100 us (98%)
  local copies, waits for them, and re-layouts  1.32 us (1%)
    pallas_call x1, Pallas kernels, body(): pl.pallas_call(kernel, out_shape=pltpu.VMEM((RB * BS, b_matrix.shape[1]),...  100 us

profile of v2, /device:TPU:1, one launch (start us, length us, event | category | flops | bytes accessed | tf_op | source)
XLA Modules:
  0.0 101.7 jit_solution(14294796525342718172)
XLA Ops:
  0.0 100.3 %shard_map.64 = bf16[1024,1024]{1,0:T(8,128)(2,1)S(1)} custom-call(bf16[32,128,128]{2,1,0:T(8,128)(2,1)} %bitcast.8, s32[2,16]{1,0:T(2,128)} %bitcast.9, s32[2,16]{1,0:T(2,128)} %bitcast.10, s32[1,16]{1,0:T(1,128)} %bitcast.11, s32[1,8]{1,0:T(1,128)} %owned_ref.1, bf16[512,1024]{1,0:T(8,128)(2,1)} %b_ref.1), custom_call_target="tpu_custom_call" | custom-call | tf_op jit(solution)/shard_map/pallas_call | solution.py:508
  100.4 1.3 %copy.8 = bf16[1024,1024]{1,0:T(8,128)(2,1)} copy(bf16[1024,1024]{1,0:T(8,128)(2,1)S(1)} %shard_map.64) | data formatting | bytes 4194304

commit v3 on v2

--- a/solution.py
+++ b/solution.py
@@ -13,7 +13,7 @@
 WIDTH = (256, 256)
 LEFT = (0, 256)
 CH = 16
-SF = 12
+SF = 10
 R1 = 288
 ROWS = 512
 NONE = 256
@@ -435,28 +435,31 @@
     meta_start()
     pgot(("pa", 0), item(1, "Q", b))
     x_full(1, "Q")
+    x_last(0, "Q")
+    b_step1(1)
     find_all()
-    x_last(0, "Q")
     for i in "OQ":
         c_end(0, i)
+    b_step2(1)
     b_got_q(0, 0)
     add(0, 0, 0)
+    x_fwd(1, "O")
     b_got_q(0, 1)
     add(0, 0, 1)
-    b_step1(1)
     b_got_q(0, 2)
     add(0, 0, 2)
+    x_fwd(1, "Q")
     b_got_q(0, 3)
     swap(0)
-    x_fwd(1, "O")
-    b_step2(1)
     p_rest_got()
-    x_fwd(1, "Q")
+    b_step3(1)
     x_last(1, "O")
-    b_step3(1)
-    for q in range(3):
-        b_got_q(1, q)
-        add(0, 1, q)
+    b_got_q(1, 0)
+    add(0, 1, 0)
+    b_got_q(1, 1)
+    add(0, 1, 1)
+    b_got_q(1, 2)
+    add(0, 1, 2)
     x_last(1, "Q")
     b_got_q(1, 3)
     swap(1)
@@ -464,9 +467,14 @@
     for i in "OQ":
         c_end(1, i)
     c_rest_end()
-    for n in (0, 1):
-        for q in range(4):
-            add(1, n, q)
+    add(1, 0, 0)
+    add(1, 0, 1)
+    add(1, 0, 2)
+    add(1, 0, 3)
+    add(1, 1, 0)
+    add(1, 1, 1)
+    add(1, 1, 2)
+    add(1, 1, 3)
 
     for j, (n, lo, hi) in enumerate(SWAPS):
         arrive(o_ref.at[pl.ds(lo * BS, (hi - lo) * BS), b_cols(t, n)], outr.at[j])

time: 102 us -> 94.7 us (0.928)
  Pallas kernels: 100 us -> 92.8 us
    pallas_call x1, Pallas kernels: 100 us -> 92.8 us  [body(): pl.pallas_call(kernel, out_shape=pltpu.VMEM((RB * BS, b_matrix.shape[1]),...]
where the time goes in v3:
time: 94.7 us; the launch traced here: 94.1 us
  Pallas kernels  92.8 us (98%)
  local copies, waits for them, and re-layouts  1.32 us (1%)
    pallas_call x1, Pallas kernels, body(): pl.pallas_call(kernel, out_shape=pltpu.VMEM((RB * BS, b_matrix.shape[1]),...  92.8 us

profile of v3, /device:TPU:1, one launch (start us, length us, event | category | flops | bytes accessed | tf_op | source)
XLA Modules:
  0.0 94.1 jit_solution(13477115654002741112)
XLA Ops:
  0.0 92.8 %shard_map.64 = bf16[1024,1024]{1,0:T(8,128)(2,1)S(1)} custom-call(bf16[32,128,128]{2,1,0:T(8,128)(2,1)} %bitcast.8, s32[2,16]{1,0:T(2,128)} %bitcast.9, s32[2,16]{1,0:T(2,128)} %bitcast.10, s32[1,16]{1,0:T(1,128)} %bitcast.11, s32[1,8]{1,0:T(1,128)} %owned_ref.1, bf16[512,1024]{1,0:T(8,128)(2,1)} %b_ref.1), custom_call_target="tpu_custom_call" | custom-call | tf_op jit(solution)/shard_map/pallas_call | solution.py:516
  92.8 1.3 %copy.8 = bf16[1024,1024]{1,0:T(8,128)(2,1)} copy(bf16[1024,1024]{1,0:T(8,128)(2,1)S(1)} %shard_map.64) | data formatting | bytes 4194304

commit v4 on v3

--- a/solution.py
+++ b/solution.py
@@ -13,7 +13,7 @@
 WIDTH = (256, 256)
 LEFT = (0, 256)
 CH = 16
-SF = 10
+SF = 9
 R1 = 288
 ROWS = 512
 NONE = 256
@@ -196,7 +196,6 @@
     def b_cols(side_at, n):
         return pl.ds(pl.multiple_of(side_at * 512 + LEFT[n], 128), WIDTH[n])
 
-    a_send(0)
     own_b, cross_b = [], []
     for n in (0, 1):
         cp = pltpu.make_async_copy(b_ref.at[:, b_cols(t, n)], bx[n], loc.at[n])
@@ -206,10 +205,12 @@
         cp = pltpu.make_async_copy(b_ref.at[:, b_cols(s, n)], bp[n].at[kown], loc.at[2 + n])
         cp.start()
         own_b.append(cp)
+    a_send(0)
     for n in (0, 1):
         cross_b[n].wait()
         i = B_LABELS.at[(n, "cross")]
         start(bx[n], bp[n].at[kown], bs.at[i], br.at[i], pair)
+    a_send(1)
 
     @pl.loop(1, 16)
     def _(j):
@@ -396,7 +397,6 @@
         start(outp[n].at[rows], o_ref.at[rows, b_cols(s, n)], outs.at[j], outr.at[j], pair)
 
     x_pieces((0, 1, 2, 3))
-    a_send(1)
     x_pieces((4, 5, 6, 7))
     csend((0, "O", "own"), item(0, "O", b))
     b_start(0)

time: 94.7 us -> 94.8 us (level); the launches traced: 94.1 us -> 93 us
  Pallas kernels: 92.8 us -> 91.7 us
    pallas_call x1, Pallas kernels: 92.8 us -> 91.7 us  [body(): pl.pallas_call(kernel, out_shape=pltpu.VMEM((RB * BS, b_matrix.shape[1]),...]
where the time goes in v4:
time: 94.8 us; the launch traced here: 93 us
  Pallas kernels  91.7 us (97%)
  local copies, waits for them, and re-layouts  1.32 us (1%)
    pallas_call x1, Pallas kernels, body(): pl.pallas_call(kernel, out_shape=pltpu.VMEM((RB * BS, b_matrix.shape[1]),...  91.7 us

profile of v4, /device:TPU:1, one launch (start us, length us, event | category | flops | bytes accessed | tf_op | source)
XLA Modules:
  0.0 93.0 jit_solution(18211335872238360139)
XLA Ops:
  0.0 91.7 %shard_map.64 = bf16[1024,1024]{1,0:T(8,128)(2,1)S(1)} custom-call(bf16[32,128,128]{2,1,0:T(8,128)(2,1)} %bitcast.8, s32[2,16]{1,0:T(2,128)} %bitcast.9, s32[2,16]{1,0:T(2,128)} %bitcast.10, s32[1,16]{1,0:T(1,128)} %bitcast.11, s32[1,8]{1,0:T(1,128)} %owned_ref.1, bf16[512,1024]{1,0:T(8,128)(2,1)} %b_ref.1), custom_call_target="tpu_custom_call" | custom-call | tf_op jit(solution)/shard_map/pallas_call | solution.py:516
  91.7 1.3 %copy.8 = bf16[1024,1024]{1,0:T(8,128)(2,1)} copy(bf16[1024,1024]{1,0:T(8,128)(2,1)S(1)} %shard_map.64) | data formatting | bytes 4194304
